TPU v7x, 128 devices: a whole 4x4x4 slice. The times are simulated.
128 devices in a mesh: row: 8 (over z, core), col: 16 (over y, x).
Axes of the slice: x: 4, y: 4, z: 4, core: 2. Of those that a mesh axis runs over, the one named last changes fastest.
Arguments:
- inverse: bfloat16 [18432, 18432], P('row', 'col'), may hold values from -0.046875 to 0.046875
- pair_block: bfloat16 [18432, 2560], P('row', 'col'), may hold values from -6 to 6
- coeffs: bfloat16 [5120, 2560], P('row'), may hold values from -0.125 to 0.125
Outputs:
- gradient_ao: bfloat16 [18432, 5120], P('col', 'row')
All inputs are finite; a program needn't handle non-finite values.
Results may differ from a plain program's by a relative error of at most 0.0049.
Values may be sent and summed in bfloat16 or wider, within the bound.
A program may use at most 128 MiB of HBM per device.

v0:
```python
import jax
import jax.numpy as jnp
from jax import lax
from jax.sharding import PartitionSpec as P


def shards(inverse, pair_block, coeffs):
    cols_here = inverse.shape[1]
    row_count = lax.axis_size("row")
    col_count = lax.axis_size("col")
    blocks_per = col_count // row_count
    col_index = lax.axis_index("col")
    row_index = lax.axis_index("row")
    offset_rows = col_index % blocks_per * cols_here
    holds_diag = col_index // blocks_per == row_index
    columns = lax.all_gather(pair_block, "col", axis=1, tiled=True)
    product = lax.dot_general(
        inverse, columns, (((0,), (0,)), ((), ())), preferred_element_type=jnp.float32
    )
    diagonal = lax.dynamic_slice_in_dim(columns, offset_rows, cols_here, 0).astype(jnp.float32)
    partial_value = product - jnp.where(holds_diag, diagonal, jnp.zeros_like(diagonal))
    portion = lax.psum_scatter(partial_value, "row", scatter_dimension=1, tiled=True)
    gamma_aux = lax.all_gather(portion.astype(jnp.bfloat16), "row", axis=1, tiled=True)
    result = lax.dot_general(
        gamma_aux, coeffs, (((1,), (1,)), ((), ())), preferred_element_type=jnp.float32
    )
    return result.astype(jnp.bfloat16)


def solution(mesh):
    placed = (P("row", "col"), P("row", "col"), P("row", None))
    return jax.shard_map(
        shards, mesh=mesh, in_specs=placed, out_specs=P("col", "row"), check_vma=False
    )
```

profile of v0, /device:TPU:1, one launch (start us, length us, event | category | flops | bytes accessed | tf_op | source)
XLA Modules:
  0.0 247.1 jit_solution(13387108250398124115)
XLA Ops:
  6.5 0.0 copy-start
  6.5 0.0 all-gather.3.cloned.1.call-start
  6.5 0.7 all-gather.3.cloned.1.call-update
  7.3 0.0 reduce-scatter.2.cloned.1.call-start
  7.3 91.7 %all-gather.3.cloned.1.call-done = bf16[2304,2560]{0,1:T(8,128)(2,1)} async-done(((bf16[2304,160]{0,1:T(8,128)(2,1)}), bf16[2304,2560]{0,1:T(8,128)(2,1)}) %all-gather.3.cloned.1.call-update) | async-done | bytes 11796496 | tf_op jit(solution)/shard_map/all_gather | solution.py:16
  99.0 22.4 %convolution_subtract_fusion = f32[1152,2560]{0,1:T(8,128)} fusion(bf16[2304,2560]{0,1:T(8,128)(2,1)} %all-gather.3.cloned.1.call-done, bf16[2304,1152]{1,0:T(8,128)(2,1)} %param.3, s32[]{:T(128)S(6)} %select_n.25, pred[]{:T(512)S(6)} %eq.5), kind=kOutput, calls=%fused_computation | convolution fusion | flops 13598392320 | bytes 34799620 | tf_op jit(solution)/shard_map/dot_general | solution.py:17
  121.4 0.0 reduce-scatter.2.cloned.1.call-update
  121.4 0.0 all-gather.5.cloned.1.call-start
  121.5 68.0 %reduce-scatter.2.cloned.1.call-done = f32[1152,320]{0,1:T(8,128)} async-done(((f32[1152,2560]{0,1:T(8,128)}), f32[1152,320]{0,1:T(8,128)}) %reduce-scatter.2.cloned.1.call-update) | async-done | bytes 1474576 | tf_op jit(solution)/shard_map/reduce_scatter | solution.py:22
  189.5 2.3 convert_element_type.10
  191.8 0.0 all-gather.5.cloned.1.call-update
  191.8 40.2 %all-gather.5.cloned.1.call-done = bf16[1152,2560]{0,1:T(8,128)(2,1)} async-done(((bf16[1152,320]{0,1:T(8,128)(2,1)}), bf16[1152,2560]{0,1:T(8,128)(2,1)}) %all-gather.5.cloned.1.call-update) | async-done | bytes 5898256 | tf_op jit(solution)/shard_map/all_gather | solution.py:23
  232.0 0.0 copy-done
  232.0 8.6 %convolution_convert_fusion = bf16[1152,640]{1,0:T(8,128)(2,1)} fusion(bf16[1152,2560]{0,1:T(8,128)(2,1)} %all-gather.5.cloned.1.call-done, bf16[640,2560]{1,0:T(8,128)(2,1)S(1)} %copy-done), kind=kOutput, calls=%fused_computation.1 | convolution fusion | flops 3775610880 | bytes 10649600 | tf_op jit(solution)/shard_map/dot_general | solution.py:24
Async XLA Ops:
  6.5 225.5 %copy-start = (bf16[640,2560]{1,0:T(8,128)(2,1)S(1)}, bf16[640,2560]{1,0:T(8,128)(2,1)}, u32[]{:S(2)}) copy-start(bf16[640,2560]{1,0:T(8,128)(2,1)} %param.5) | copy-start | bytes 9830404
  6.5 92.5 %all-gather.3.cloned.1.call-start = ((), (), s32[]{:S(2)}) async-start(), calls=%async_computation.1 | async-start | bytes 12533760 | tf_op jit(solution)/shard_map/all_gather | solution.py:16
  7.3 182.2 %reduce-scatter.2.cloned.1.call-start = ((), (), s32[]{:S(2)}) async-start(), calls=%async_computation.2 | async-start | bytes 13271040 | tf_op jit(solution)/shard_map/reduce_scatter | solution.py:22
  121.4 110.6 %all-gather.5.cloned.1.call-start = ((), (), s32[]{:S(2)}) async-start(), calls=%async_computation.3 | async-start | bytes 6635520 | tf_op jit(solution)/shard_map/all_gather | solution.py:23
Sparse Core Ops, SparseCore 0:
  9.5 89.5 all-gather.2
  121.6 67.8 reduce-scatter.1
  191.9 40.0 all-gather.4
where the time goes:
time: 247 us
  waiting for transfers between devices  201 us (81%)
  matrix products  31 us (13%)
  between operations  13.1 us (5%)
    all_gather x1, waiting for transfers between devices, shards(): columns = lax.all_gather(pair_block, 'col', axis=1, tiled=True)  91.7 us
    reduce_scatter x1, waiting for transfers between devices, shards(): lax.psum_scatter(partial_value, 'row', scatter_dimension=1, tiled=True)  68 us
    all_gather x1, waiting for transfers between devices, shards(): lax.all_gather(portion.astype(jnp.bfloat16), 'row', axis=1, tiled=True)  40.2 us
    dot_general x1, matrix products, shards(): lax.dot_general(inverse, columns, (((0,), (0,)), ((), ())), preferred_ele...  22.4 us
    dot_general x1, matrix products, shards(): lax.dot_general(gamma_aux, coeffs, (((1,), (1,)), ((), ())), preferred_el...  8.58 us
  transfers between devices with their start and end apart: 3, of which 3 were waited for; matrix products, arithmetic and copies ran while one was open for 0% of the time, Pallas kernels for 0%

commit v1 on v0

--- a/solution.py
+++ b/solution.py
@@ -13,7 +13,15 @@
     row_index = lax.axis_index("row")
     offset_rows = col_index % blocks_per * cols_here
     holds_diag = col_index // blocks_per == row_index
-    columns = lax.all_gather(pair_block, "col", axis=1, tiled=True)
+    ways, here = (lax.axis_size("col"), lax.axis_index("col"))
+    grown, reach = (pair_block, 1)
+    while reach < ways:
+        theirs = lax.ppermute(grown, "col", [(d, d ^ reach) for d in range(ways)])
+        mine_first = jnp.concatenate([grown, theirs], axis=1)
+        theirs_first = jnp.concatenate([theirs, grown], axis=1)
+        grown = jnp.where(here & reach == 0, mine_first, theirs_first)
+        reach = 2 * reach
+    columns = grown
     product = lax.dot_general(
         inverse, columns, (((0,), (0,)), ((), ())), preferred_element_type=jnp.float32
     )

time: 247 us -> 428 us (1.73)
  waiting for transfers between devices: 201 us -> 348 us
  other arithmetic: 2.31 us -> 28 us
  starting transfers between devices: 0.08 us -> 9.79 us
    ppermute x0 -> x4, waiting for transfers between devices: none -> 233 us  [shards(): theirs = lax.ppermute(grown, 'col', [(d, d ^ reach) for d in range(ways)])]
    all_gather x1 -> x0, waiting for transfers between devices: 91.7 us -> none  [shards(): columns = lax.all_gather(pair_block, 'col', axis=1, tiled=True)]
    select_n x0 -> x4, other arithmetic: none -> 25.6 us  [shards(): grown = jnp.where(here & reach == 0, mine_first, theirs_first)]
    ppermute x0 -> x4, starting transfers between devices: none -> 9.75 us  [shards(): theirs = lax.ppermute(grown, 'col', [(d, d ^ reach) for d in range(ways)])]
    reduce_scatter x1, waiting for transfers between devices: 68 us -> 74.2 us  [shards(): lax.psum_scatter(partial_value, 'row', scatter_dimension=1, tiled=True)]
  transfers between devices with their start and end apart: 3 -> 6, of which waited for: 3 -> 6; matrix products, arithmetic and copies ran while one was open for 0% -> 0% of each run, Pallas kernels for 0% -> 0%
where the time goes in v1:
time: 428 us; the launch traced here: 427 us
  waiting for transfers between devices  348 us (81%)
  matrix products  28.7 us (7%)
  other arithmetic  28 us (7%)
  between operations  13.4 us (3%)
  starting transfers between devices  9.79 us (2%)
    ppermute x4, waiting for transfers between devices, shards(): theirs = lax.ppermute(grown, 'col', [(d, d ^ reach) for d in range(ways)])  233 us
    reduce_scatter x1, waiting for transfers between devices, shards(): lax.psum_scatter(partial_value, 'row', scatter_dimension=1, tiled=True)  74.2 us
    all_gather x1, waiting for transfers between devices, shards(): lax.all_gather(portion.astype(jnp.bfloat16), 'row', axis=1, tiled=True)  40.2 us
    select_n x4, other arithmetic, shards(): grown = jnp.where(here & reach == 0, mine_first, theirs_first)  25.6 us
    dot_general x1, matrix products, shards(): lax.dot_general(inverse, columns, (((0,), (0,)), ((), ())), preferred_ele...  20.1 us
    ppermute x4, starting transfers between devices, shards(): theirs = lax.ppermute(grown, 'col', [(d, d ^ reach) for d in range(ways)])  9.75 us
    dot_general x1, matrix products, shards(): lax.dot_general(gamma_aux, coeffs, (((1,), (1,)), ((), ())), preferred_el...  8.58 us
  transfers between devices with their start and end apart: 6, of which 6 were waited for; matrix products, arithmetic and copies ran while one was open for 0% of the time, Pallas kernels for 0%

profile of v1, /device:TPU:1, one launch (start us, length us, event | category | flops | bytes accessed | tf_op | source)
XLA Modules:
  0.0 427.4 jit_solution(7814513795699739893)
XLA Ops:
  6.5 0.0 copy-start
  6.5 0.0 reduce-scatter.2.cloned.1.call-start
  6.5 2.0 collective-permute-start
  8.6 16.0 %collective-permute-done = bf16[2304,160]{0,1:T(8,128)(2,1)} collective-permute-done((bf16[2304,160]{0,1:T(8,128)(2,1)}, bf16[2304,160]{0,1:T(8,128)(2,1)}, u32[]{:S(2)}, u32[]{:S(2)}) %collective-permute-start) | collective-permute-done | bytes 737312 | tf_op jit(solution)/shard_map/ppermute | solution.py:19
  24.6 3.3 maximum_select_fusion.3
  27.9 3.2 collective-permute-start.1
  31.1 31.1 %collective-permute-done.1 = bf16[2304,320]{0,1:T(8,128)(2,1)} collective-permute-done((bf16[2304,320]{0,1:T(8,128)(2,1)}, bf16[2304,320]{0,1:T(8,128)(2,1)}, u32[]{:S(2)}, u32[]{:S(2)}) %collective-permute-start.1) | collective-permute-done | bytes 1474592 | tf_op jit(solution)/shard_map/ppermute | solution.py:19
  62.3 4.2 maximum_select_fusion.2
  66.4 1.5 collective-permute-start.2
  67.9 61.8 %collective-permute-done.2 = bf16[2304,640]{0,1:T(8,128)(2,1)} collective-permute-done((bf16[2304,640]{0,1:T(8,128)(2,1)}, bf16[2304,640]{0,1:T(8,128)(2,1)}, u32[]{:S(2)}, u32[]{:S(2)}) %collective-permute-start.2) | collective-permute-done | bytes 2949152 | tf_op jit(solution)/shard_map/ppermute | solution.py:19
  129.8 8.3 %maximum_select_fusion.1 = bf16[2304,1280]{0,1:T(8,128)(2,1)} fusion(bf16[2304,640]{0,1:T(8,128)(2,1)} %collective-permute-done.2, bf16[2304,640]{0,1:T(8,128)(2,1)} %maximum_select_fusion.2, pred[]{:T(512)S(6)} %eq.18), kind=kLoop, calls=%fused_computation.3 | loop fusion | flops 26542080 | bytes 11796481 | tf_op jit(solution)/shard_map/jit(_where)/select_n | solution.py:22
  138.1 3.0 collective-permute-start.3
  141.1 124.2 %collective-permute-done.3 = bf16[2304,1280]{0,1:T(8,128)(2,1)} collective-permute-done((bf16[2304,1280]{0,1:T(8,128)(2,1)}, bf16[2304,1280]{0,1:T(8,128)(2,1)}, u32[]{:S(2)}, u32[]{:S(2)}) %collective-permute-start.3) | collective-permute-done | bytes 5898272 | tf_op jit(solution)/shard_map/ppermute | solution.py:19
  265.2 9.8 %maximum_select_fusion = bf16[2304,2560]{0,1:T(8,128)(2,1)S(1)} fusion(bf16[2304,1280]{0,1:T(8,128)(2,1)} %collective-permute-done.3, bf16[2304,1280]{0,1:T(8,128)(2,1)} %maximum_select_fusion.1, pred[]{:T(512)S(6)} %eq.17), kind=kLoop, calls=%fused_computation.2 | loop fusion | flops 53084160 | bytes 23592960 | tf_op jit(solution)/shard_map/jit(_where)/select_n | solution.py:22
  275.0 20.1 %fusion = f32[1152,2560]{0,1:T(8,128)} fusion(bf16[2304,2560]{0,1:T(8,128)(2,1)S(1)} %maximum_select_fusion, bf16[2304,1152]{1,0:T(8,128)(2,1)} %param.3, s32[]{:T(128)S(6)} %select_n.65, pred[]{:T(512)S(6)} %eq.21), kind=kOutput, calls=%fused_computation.1 | convolution fusion | flops 13598392320 | bytes 34799620 | tf_op jit(solution)/shard_map/dot_general | solution.py:25
  295.1 0.0 reduce-scatter.2.cloned.1.call-update
  295.1 0.0 all-gather.2.cloned.1.call-start
  295.2 74.2 %reduce-scatter.2.cloned.1.call-done = f32[1152,320]{0,1:T(8,128)} async-done(((f32[1152,2560]{0,1:T(8,128)}), f32[1152,320]{0,1:T(8,128)}) %reduce-scatter.2.cloned.1.call-update) | async-done | bytes 1474576 | tf_op jit(solution)/shard_map/reduce_scatter | solution.py:30
  369.4 2.3 convert_element_type.10
  371.7 0.0 all-gather.2.cloned.1.call-update
  371.7 40.2 %all-gather.2.cloned.1.call-done = bf16[1152,2560]{0,1:T(8,128)(2,1)} async-done(((bf16[1152,320]{0,1:T(8,128)(2,1)}), bf16[1152,2560]{0,1:T(8,128)(2,1)}) %all-gather.2.cloned.1.call-update) | async-done | bytes 5898256 | tf_op jit(solution)/shard_map/all_gather | solution.py:31
  412.0 0.0 copy-done
  412.0 8.6 %convolution_convert_fusion = bf16[1152,640]{1,0:T(8,128)(2,1)} fusion(bf16[1152,2560]{0,1:T(8,128)(2,1)} %all-gather.2.cloned.1.call-done, bf16[640,2560]{1,0:T(8,128)(2,1)S(1)} %copy-done), kind=kOutput, calls=%fused_computation.4 | convolution fusion | flops 3775610880 | bytes 10649600 | tf_op jit(solution)/shard_map/dot_general | solution.py:32
Async XLA Ops:
  6.5 405.4 %copy-start = (bf16[640,2560]{1,0:T(8,128)(2,1)S(1)}, bf16[640,2560]{1,0:T(8,128)(2,1)}, u32[]{:S(2)}) copy-start(bf16[640,2560]{1,0:T(8,128)(2,1)} %param.5) | copy-start | bytes 9830404
  6.5 362.9 %reduce-scatter.2.cloned.1.call-start = ((), (), s32[]{:S(2)}) async-start(), calls=%async_computation.1 | async-start | bytes 13271040 | tf_op jit(solution)/shard_map/reduce_scatter | solution.py:30
  6.5 18.1 %collective-permute-start = (bf16[2304,160]{0,1:T(8,128)(2,1)}, bf16[2304,160]{0,1:T(8,128)(2,1)}, u32[]{:S(2)}, u32[]{:S(2)}) collective-permute-start(bf16[2304,160]{0,1:T(8,128)(2,1)} %param.4), channel_id=1, source_target_pairs={{0,1},{1,0},{2,3},{3,2},{4,5},{5,4},{6,7},{7,6},{8,9},{9,8},{10,11... | collective-permute-start | bytes 2211848 | tf_op jit(solution)/shard_map/ppermute | solution.py:19
  27.9 34.3 %collective-permute-start.1 = (bf16[2304,320]{0,1:T(8,128)(2,1)}, bf16[2304,320]{0,1:T(8,128)(2,1)}, u32[]{:S(2)}, u32[]{:S(2)}) collective-permute-start(bf16[2304,320]{0,1:T(8,128)(2,1)} %maximum_select_fusion.3), channel_id=1, source_target_pairs={{0,2},{1,3},{2,0},{3,1},{4,6},{5,7},{6,4},{7,5},{8,10},{9,11},{10,... | collective-permute-start | bytes 4423688 | tf_op jit(solution)/shard_map/ppermute | solution.py:19
  66.4 63.3 %collective-permute-start.2 = (bf16[2304,640]{0,1:T(8,128)(2,1)}, bf16[2304,640]{0,1:T(8,128)(2,1)}, u32[]{:S(2)}, u32[]{:S(2)}) collective-permute-start(bf16[2304,640]{0,1:T(8,128)(2,1)} %maximum_select_fusion.2), channel_id=1, source_target_pairs={{0,4},{1,5},{2,6},{3,7},{4,0},{5,1},{6,2},{7,3},{8,12},{9,13},{10,... | collective-permute-start | bytes 8847368 | tf_op jit(solution)/shard_map/ppermute | solution.py:19
  138.1 127.2 %collective-permute-start.3 = (bf16[2304,1280]{0,1:T(8,128)(2,1)}, bf16[2304,1280]{0,1:T(8,128)(2,1)}, u32[]{:S(2)}, u32[]{:S(2)}) collective-permute-start(bf16[2304,1280]{0,1:T(8,128)(2,1)} %maximum_select_fusion.1), channel_id=1, source_target_pairs={{0,8},{1,9},{2,10},{3,11},{4,12},{5,13},{6,14},{7,15},{8,0},{9,1},... | collective-permute-start | bytes 17694728 | tf_op jit(solution)/shard_map/ppermute | solution.py:19
  295.1 116.8 %all-gather.2.cloned.1.call-start = ((), (), s32[]{:S(2)}) async-start(), calls=%async_computation.2 | async-start | bytes 6635520 | tf_op jit(solution)/shard_map/all_gather | solution.py:31
Sparse Core Ops, SparseCore 0:
  295.3 74.0 reduce-scatter.1
  371.9 40.0 all-gather.1
